TPU v7x, 32 devices: a whole 2x2x4 slice. The times are simulated.
32 devices in a mesh: gx: 2 (over core), gy: 4 (over y, x), gz: 4 (over z).
Axes of the slice: x: 2, y: 2, z: 4, core: 2. Of those that a mesh axis runs over, the one named last changes fastest.
Arguments:
- student: bfloat16 [1024, 1024], P('gx', 'gz'), may hold values from -12 to 12
- teacher: bfloat16 [8192, 1024], P('gy', 'gz'), may hold values from -6 to 6
- block_ids: int32 [8, 32], P('gx'), may hold values from 0 to 63, as said below
- block_valid: int32 [8, 32], P('gx'), may hold values from 0 to 1
Outputs:
- row_potential: float32 [1024], P('gx')
- column_potential: float32 [8192], P('gy')
Inputs may be any that keep to these rules, and one draw needn't show every extreme that they name: `block_ids`: within each row block the valid slots name distinct column blocks, and at most 8 of them lie in one aligned group of 16 column blocks; in every draw some row block has exactly 8 valid slots in one group.
All inputs are finite; a program needn't handle non-finite values.
Results may differ from a plain program's by a relative error of at most 0.0003.
Values sent between devices are 32-bit elements; how exact they have to be, the bound alone decides.
A program may use at most 64 MiB of HBM per device.

v0:
```python
import math
import jax
import jax.numpy as jnp
from jax import lax
from jax.sharding import PartitionSpec as P

F = 1024
TILE = 128
LOCAL_MOST = 8
ITERS = 5
SOFTNESS = 0.1
EXACT = lax.Precision.HIGHEST


def combined_all(x, axis, combine):
    everything = jax.tree.map(lambda part: lax.all_gather(part, axis), x)
    initial = jax.tree.map(lambda part: part[0], everything)

    def lap(k, so_far):
        return combine(so_far, jax.tree.map(lambda part: part[k], everything))

    return lax.fori_loop(1, lax.axis_size(axis), lap, initial)


def soft_bound(highest, totals):
    return -SOFTNESS * (highest + jnp.log(totals + jnp.exp(-highest)))


def pair_merge(earlier, later):
    highest = jnp.maximum(earlier[0], later[0])
    return (
        highest,
        earlier[1] * jnp.exp(earlier[0] - highest) + later[1] * jnp.exp(later[0] - highest),
    )


def row_partial(costs, column_values, one_hot, live_mask):
    gathered = jnp.einsum("rmb,bw->rmw", one_hot, column_values, precision=EXACT)
    scores = (gathered[:, :, :, None] - costs) / SOFTNESS
    highest = jnp.maximum(jnp.max(jnp.where(live_mask, scores, -1e30), axis=(1, 2)), 0.0)
    totals = jnp.sum(
        jnp.where(live_mask, jnp.exp(scores - highest[:, None, None, :]), 0.0), axis=(1, 2)
    )
    return (highest, totals)


def local_totals(scores, highest, one_hot, live_mask):
    chosen_peak = jnp.einsum("rmb,bw->rmw", one_hot, highest, precision=EXACT)
    tile_sum = jnp.sum(
        jnp.where(live_mask, jnp.exp(scores - chosen_peak[:, :, :, None]), 0.0), axis=3
    )
    return jnp.einsum("rmb,rmw->bw", one_hot, tile_sum, precision=EXACT)


def column_update(costs, row_values, one_hot, live_mask):
    scores = (row_values[:, None, None, :] - costs) / SOFTNESS
    tile_peak = jnp.max(scores, axis=3)
    spread_peak = jnp.where(one_hot[:, :, :, None] > 0, tile_peak[:, :, None, :], 0.0)
    local_peak = jnp.maximum(jnp.max(spread_peak, axis=(0, 1)), 0.0)
    partial_sum = local_totals(scores, local_peak, one_hot, live_mask)
    highest, totals = combined_all((local_peak, partial_sum), "gx", pair_merge)
    return soft_bound(highest, totals)


def on_device(student, teacher, block_ids, block_valid):
    span_blocks = teacher.shape[0] // TILE
    width_part = student.shape[1]
    column_index = lax.axis_index("gy")
    local_ids = block_ids - column_index * span_blocks
    owned = (block_valid > 0) & (local_ids >= 0) & (local_ids < span_blocks)
    slot_rank = jnp.cumsum(owned.astype(jnp.int32), axis=1) - 1
    slot_range = jnp.arange(LOCAL_MOST, dtype=jnp.int32)
    chosen_slots = (
        owned[:, None, :] & (slot_rank[:, None, :] == slot_range[None, :, None])
    ).astype(jnp.int32)
    live_slots = jnp.sum(chosen_slots, axis=2)
    block_of = jnp.sum(chosen_slots * local_ids[:, None, :], axis=2)
    block_range = jnp.arange(span_blocks, dtype=jnp.int32)
    one_hot = (
        (block_of[:, :, None] == block_range[None, None, :]) & (live_slots[:, :, None] > 0)
    ).astype(jnp.float32)
    live_mask = (live_slots > 0)[:, :, None, None]
    teacher_blocks = teacher.reshape(span_blocks, TILE, width_part)
    student_blocks = student.reshape(-1, TILE, width_part)
    picked = teacher_blocks[block_of]
    partial_dots = jnp.einsum(
        "rmcf,rif->rmci", picked, student_blocks, preferred_element_type=jnp.float32
    )
    cost_scale = -1.0 / math.sqrt(F)
    costs = lax.psum(partial_dots, "gz") * cost_scale
    column_values = jnp.zeros((span_blocks, costs.shape[2]), jnp.float32)
    row_values = jnp.zeros((student_blocks.shape[0], TILE), jnp.float32)
    for sweep in range(ITERS):
        highest, totals = row_partial(costs, column_values, one_hot, live_mask)
        highest, totals = combined_all((highest, totals), "gy", pair_merge)
        row_values = soft_bound(highest, totals)
        column_values = column_update(costs, row_values, one_hot, live_mask)
    return (row_values.reshape(-1), column_values.reshape(-1))


def solution(mesh):
    placed = (P("gx", "gz"), P("gy", "gz"), P("gx", None), P("gx", None))
    return jax.shard_map(
        on_device, mesh=mesh, in_specs=placed, out_specs=(P("gx"), P("gy")), check_vma=False
    )
```

profile of v0, /device:TPU:0, one launch (start us, length us, event | category | flops | bytes accessed | tf_op | source)
XLA Modules:
  0.0 226.9 jit_solution(7999439772396991120)
XLA Ops:
  7.2 0.8 fusion.164
  9.5 2.0 fusion.165
  11.8 88.7 %all-reduce.2.cloned.1.call-done = f32[4,8,128,128]{3,2,1,0:T(8,128)} async-done(((f32[4,8,128,128]{3,2,1,0:T(8,128)}), f32[4,8,128,128]{3,2,1,0:T(8,128)}) %all-reduce.2.cloned.1.call-update) | async-done | bytes 2097168 | tf_op jit(solution)/shard_map/psum | solution.py:90
  100.6 2.1 select_reduce_fusion.14
  103.6 8.1 %all-gather.21 = f32[4,4,128]{2,1,0:T(4,128)S(1)} all-gather(f32[1,4,128]{2,1,0:T(4,128)S(1)} %bitcast.193), channel_id=3, replica_groups=mesh['gx'=2,'gy'=4,'gz'=4] {'gy'}, dimensions={0}, use_global_device_ids=true | all-gather | bytes 10240 | tf_op jit(solution)/shard_map/all_gather | solution.py:16
  111.6 8.0 %all-gather.20 = f32[4,4,128]{2,1,0:T(4,128)S(1)} all-gather(f32[1,4,128]{2,1,0:T(4,128)S(1)} %get-tuple-element.841), channel_id=2, replica_groups=mesh['gx'=2,'gy'=4,'gz'=4] {'gy'}, dimensions={0}, use_global_device_ids=true | all-gather | bytes 10240 | tf_op jit(solution)/shard_map/all_gather | solution.py:16
  120.8 1.3 select_reduce_fusion.12
  122.4 1.8 all-gather.3
  124.2 1.8 all-gather.2
  127.0 0.8 select_reduce_fusion.10
  127.8 7.1 %all-gather.23 = f32[4,4,128]{2,1,0:T(4,128)S(1)} all-gather(f32[1,4,128]{2,1,0:T(4,128)S(1)} %bitcast.194), channel_id=7, replica_groups=mesh['gx'=2,'gy'=4,'gz'=4] {'gy'}, dimensions={0}, use_global_device_ids=true | all-gather | bytes 10240 | tf_op jit(solution)/shard_map/all_gather | solution.py:16
  134.9 8.0 %all-gather.22 = f32[4,4,128]{2,1,0:T(4,128)S(1)} all-gather(f32[1,4,128]{2,1,0:T(4,128)S(1)} %get-tuple-element.839), channel_id=6, replica_groups=mesh['gx'=2,'gy'=4,'gz'=4] {'gy'}, dimensions={0}, use_global_device_ids=true | all-gather | bytes 10240 | tf_op jit(solution)/shard_map/all_gather | solution.py:16
  144.1 1.3 select_reduce_fusion.9
  145.7 1.8 all-gather.7
  147.5 1.8 all-gather.6
  150.3 0.8 select_reduce_fusion.7
  151.1 7.1 %all-gather.25 = f32[4,4,128]{2,1,0:T(4,128)S(1)} all-gather(f32[1,4,128]{2,1,0:T(4,128)S(1)} %bitcast.195), channel_id=11, replica_groups=mesh['gx'=2,'gy'=4,'gz'=4] {'gy'}, dimensions={0}, use_global_device_ids=true | all-gather | bytes 10240 | tf_op jit(solution)/shard_map/all_gather | solution.py:16
  158.2 8.0 %all-gather.24 = f32[4,4,128]{2,1,0:T(4,128)S(1)} all-gather(f32[1,4,128]{2,1,0:T(4,128)S(1)} %get-tuple-element.837), channel_id=10, replica_groups=mesh['gx'=2,'gy'=4,'gz'=4] {'gy'}, dimensions={0}, use_global_device_ids=true | all-gather | bytes 10240 | tf_op jit(solution)/shard_map/all_gather | solution.py:16
  167.4 1.3 select_reduce_fusion.6
  169.0 1.8 all-gather.11
  170.8 1.8 all-gather.10
  173.6 0.8 select_reduce_fusion.4
  174.4 7.1 %all-gather.27 = f32[4,4,128]{2,1,0:T(4,128)S(1)} all-gather(f32[1,4,128]{2,1,0:T(4,128)S(1)} %bitcast.196), channel_id=15, replica_groups=mesh['gx'=2,'gy'=4,'gz'=4] {'gy'}, dimensions={0}, use_global_device_ids=true | all-gather | bytes 10240 | tf_op jit(solution)/shard_map/all_gather | solution.py:16
  181.5 8.0 %all-gather.26 = f32[4,4,128]{2,1,0:T(4,128)S(1)} all-gather(f32[1,4,128]{2,1,0:T(4,128)S(1)} %get-tuple-element.835), channel_id=14, replica_groups=mesh['gx'=2,'gy'=4,'gz'=4] {'gy'}, dimensions={0}, use_global_device_ids=true | all-gather | bytes 10240 | tf_op jit(solution)/shard_map/all_gather | solution.py:16
  190.7 1.3 select_reduce_fusion.3
  192.3 1.8 all-gather.15
  194.1 2.0 all-gather.14
  197.8 7.1 %all-gather.29 = f32[4,4,128]{2,1,0:T(4,128)S(1)} all-gather(f32[1,4,128]{2,1,0:T(4,128)S(1)} %bitcast.197), channel_id=19, replica_groups=mesh['gx'=2,'gy'=4,'gz'=4] {'gy'}, dimensions={0}, use_global_device_ids=true | all-gather | bytes 10240 | tf_op jit(solution)/shard_map/all_gather | solution.py:16
  205.0 8.0 %all-gather.28 = f32[4,4,128]{2,1,0:T(4,128)S(1)} all-gather(f32[1,4,128]{2,1,0:T(4,128)S(1)} %get-tuple-element.833), channel_id=18, replica_groups=mesh['gx'=2,'gy'=4,'gz'=4] {'gy'}, dimensions={0}, use_global_device_ids=true | all-gather | bytes 10240 | tf_op jit(solution)/shard_map/all_gather | solution.py:16
  214.2 1.3 select_reduce_fusion
  215.8 1.8 all-gather.19
  217.6 1.8 all-gather.18
  (96 shorter events, 15.0 us)
Async XLA Ops:
  7.2 1.4 copy-start
  7.2 93.4 %all-reduce.2.cloned.1.call-start = ((), (), s32[]{:S(2)}) async-start(), calls=%async_computation | async-start | bytes 4194304 | tf_op jit(solution)/shard_map/psum | solution.py:90
  8.6 1.0 copy-start.2
  100.6 2.2 copy-start.1
  213.2 2.3 %copy-start.3 = (f32[4,128]{1,0:T(4,128)}, f32[4,128]{1,0:T(4,128)S(1)}, u32[]{:S(2)}) copy-start(f32[4,128]{1,0:T(4,128)S(1)} %add_multiply_fusion) | copy-start | bytes 6148
Sparse Core Ops, SparseCore 0:
  11.7 88.8 all-reduce.1
where the time goes:
time: 227 us
  blocking collectives  95.1 us (42%)
  waiting for transfers between devices  88.8 us (39%)
  other arithmetic  22 us (10%)
  between operations  14.4 us (6%)
  matrix products  5.22 us (2%)
    all_gather x20, blocking collectives, combined_all(): everything = jax.tree.map(lambda part: lax.all_gather(part, axis), x)  95.1 us
    psum x1, waiting for transfers between devices, on_device(): costs = lax.psum(partial_dots, 'gz') * cost_scale  88.7 us
    reduce_sum x5, other arithmetic, local_totals(): jnp.sum(jnp.where(live_mask, jnp.exp(scores - chosen_peak[:, :, :, None])...  6.74 us
    reduce_max x5, other arithmetic, row_partial(): jnp.max(jnp.where(live_mask, scores, -1e+30), axis=(1, 2))  5.15 us
  transfers between devices with their start and end apart: 1, of which 1 were waited for; matrix products, arithmetic and copies ran while one was open for 0% of the time, Pallas kernels for 0%

commit v1 on v0

--- a/solution.py
+++ b/solution.py
@@ -87,7 +87,7 @@
         "rmcf,rif->rmci", picked, student_blocks, preferred_element_type=jnp.float32
     )
     cost_scale = -1.0 / math.sqrt(F)
-    costs = lax.psum(partial_dots, "gz") * cost_scale
+    costs = jnp.sum(lax.all_gather(partial_dots, "gz"), axis=0) * cost_scale
     column_values = jnp.zeros((span_blocks, costs.shape[2]), jnp.float32)
     row_values = jnp.zeros((student_blocks.shape[0], TILE), jnp.float32)
     for sweep in range(ITERS):

time: 227 us -> 294 us (1.30)
  waiting for transfers between devices: 88.8 us -> 152 us
  other arithmetic: 22 us -> 25 us
    all_gather x0 -> x1, waiting for transfers between devices: none -> 152 us  [on_device(): costs = jnp.sum(lax.all_gather(partial_dots, 'gz'), axis=0) * cost_scale]
    psum x1 -> x0, waiting for transfers between devices: 88.7 us -> none  [on_device(): costs = lax.psum(partial_dots, 'gz') * cost_scale]
    reduce_sum x0 -> x1, other arithmetic: none -> 4.41 us  [on_device(): costs = jnp.sum(lax.all_gather(partial_dots, 'gz'), axis=0) * cost_scale]
where the time goes in v1:
time: 294 us; the launch traced here: 293 us
  waiting for transfers between devices  152 us (52%)
  blocking collectives  95.1 us (32%)
  other arithmetic  25 us (9%)
  between operations  14.4 us (5%)
  matrix products  5.32 us (2%)
    all_gather x1, waiting for transfers between devices, on_device(): costs = jnp.sum(lax.all_gather(partial_dots, 'gz'), axis=0) * cost_scale  152 us
    all_gather x20, blocking collectives, combined_all(): everything = jax.tree.map(lambda part: lax.all_gather(part, axis), x)  95.1 us
    reduce_sum x5, other arithmetic, local_totals(): jnp.sum(jnp.where(live_mask, jnp.exp(scores - chosen_peak[:, :, :, None])...  6.74 us
  transfers between devices with their start and end apart: 1, of which 1 were waited for; matrix products, arithmetic and copies ran while one was open for 0% of the time, Pallas kernels for 0%

profile of v1, /device:TPU:0, one launch (start us, length us, event | category | flops | bytes accessed | tf_op | source)
XLA Modules:
  0.0 293.4 jit_solution(17399141005065500172)
XLA Ops:
  7.2 0.8 fusion.164
  9.5 2.1 fusion.165
  11.9 152.2 %all-gather.33.cloned.1.call-done = f32[16,8,128,128]{3,2,1,0:T(8,128)} async-done(((f32[4,8,128,128]{3,2,1,0:T(8,128)}), f32[16,8,128,128]{3,2,1,0:T(8,128)}) %all-gather.33.cloned.1.call-update) | async-done | bytes 8388624 | tf_op jit(solution)/shard_map/all_gather | solution.py:90
  164.1 4.4 %reduce_sum.122 = f32[4,8,128,128]{3,2,1,0:T(8,128)S(1)} reduce(f32[4,4,8,128,128]{4,3,2,1,0:T(8,128)} %bitcast.191, f32[]{:T(128)} %constant.253.clone.1), dimensions={0}, to_apply=%region_3.4 | reduce | flops 1572864 | bytes 10485764 | tf_op jit(solution)/shard_map/reduce_sum | solution.py:90
  169.3 0.8 select_reduce_fusion.13
  170.1 8.1 %all-gather.22 = f32[4,4,128]{2,1,0:T(4,128)S(1)} all-gather(f32[1,4,128]{2,1,0:T(4,128)S(1)} %bitcast.195), channel_id=4, replica_groups=mesh['gx'=2,'gy'=4,'gz'=4] {'gy'}, dimensions={0}, use_global_device_ids=true | all-gather | bytes 10240 | tf_op jit(solution)/shard_map/all_gather | solution.py:16
  178.2 8.0 %all-gather.21 = f32[4,4,128]{2,1,0:T(4,128)S(1)} all-gather(f32[1,4,128]{2,1,0:T(4,128)S(1)} %get-tuple-element.841), channel_id=3, replica_groups=mesh['gx'=2,'gy'=4,'gz'=4] {'gy'}, dimensions={0}, use_global_device_ids=true | all-gather | bytes 10240 | tf_op jit(solution)/shard_map/all_gather | solution.py:16
  187.3 1.3 select_reduce_fusion.12
  188.9 1.8 all-gather.4
  190.8 1.8 all-gather.3
  193.5 0.8 select_reduce_fusion.10
  194.3 7.1 %all-gather.24 = f32[4,4,128]{2,1,0:T(4,128)S(1)} all-gather(f32[1,4,128]{2,1,0:T(4,128)S(1)} %bitcast.196), channel_id=8, replica_groups=mesh['gx'=2,'gy'=4,'gz'=4] {'gy'}, dimensions={0}, use_global_device_ids=true | all-gather | bytes 10240 | tf_op jit(solution)/shard_map/all_gather | solution.py:16
  201.5 8.0 %all-gather.23 = f32[4,4,128]{2,1,0:T(4,128)S(1)} all-gather(f32[1,4,128]{2,1,0:T(4,128)S(1)} %get-tuple-element.839), channel_id=7, replica_groups=mesh['gx'=2,'gy'=4,'gz'=4] {'gy'}, dimensions={0}, use_global_device_ids=true | all-gather | bytes 10240 | tf_op jit(solution)/shard_map/all_gather | solution.py:16
  210.6 1.3 select_reduce_fusion.9
  212.2 1.8 all-gather.8
  214.1 1.8 all-gather.7
  216.8 0.8 select_reduce_fusion.7
  217.6 7.1 %all-gather.26 = f32[4,4,128]{2,1,0:T(4,128)S(1)} all-gather(f32[1,4,128]{2,1,0:T(4,128)S(1)} %bitcast.197), channel_id=12, replica_groups=mesh['gx'=2,'gy'=4,'gz'=4] {'gy'}, dimensions={0}, use_global_device_ids=true | all-gather | bytes 10240 | tf_op jit(solution)/shard_map/all_gather | solution.py:16
  224.7 8.0 %all-gather.25 = f32[4,4,128]{2,1,0:T(4,128)S(1)} all-gather(f32[1,4,128]{2,1,0:T(4,128)S(1)} %get-tuple-element.837), channel_id=11, replica_groups=mesh['gx'=2,'gy'=4,'gz'=4] {'gy'}, dimensions={0}, use_global_device_ids=true | all-gather | bytes 10240 | tf_op jit(solution)/shard_map/all_gather | solution.py:16
  233.9 1.3 select_reduce_fusion.6
  235.5 1.8 all-gather.12
  237.3 1.8 all-gather.11
  240.9 7.1 %all-gather.28 = f32[4,4,128]{2,1,0:T(4,128)S(1)} all-gather(f32[1,4,128]{2,1,0:T(4,128)S(1)} %bitcast.198), channel_id=16, replica_groups=mesh['gx'=2,'gy'=4,'gz'=4] {'gy'}, dimensions={0}, use_global_device_ids=true | all-gather | bytes 10240 | tf_op jit(solution)/shard_map/all_gather | solution.py:16
  248.0 8.2 %all-gather.27 = f32[4,4,128]{2,1,0:T(4,128)S(1)} all-gather(f32[1,4,128]{2,1,0:T(4,128)S(1)} %get-tuple-element.835), channel_id=15, replica_groups=mesh['gx'=2,'gy'=4,'gz'=4] {'gy'}, dimensions={0}, use_global_device_ids=true | all-gather | bytes 10240 | tf_op jit(solution)/shard_map/all_gather | solution.py:16
  257.4 1.3 select_reduce_fusion.3
  259.0 1.8 all-gather.16
  260.8 1.8 all-gather.15
  264.4 7.1 %all-gather.30 = f32[4,4,128]{2,1,0:T(4,128)S(1)} all-gather(f32[1,4,128]{2,1,0:T(4,128)S(1)} %bitcast.199), channel_id=20, replica_groups=mesh['gx'=2,'gy'=4,'gz'=4] {'gy'}, dimensions={0}, use_global_device_ids=true | all-gather | bytes 10240 | tf_op jit(solution)/shard_map/all_gather | solution.py:16
  271.5 8.0 %all-gather.29 = f32[4,4,128]{2,1,0:T(4,128)S(1)} all-gather(f32[1,4,128]{2,1,0:T(4,128)S(1)} %get-tuple-element.833), channel_id=19, replica_groups=mesh['gx'=2,'gy'=4,'gz'=4] {'gy'}, dimensions={0}, use_global_device_ids=true | all-gather | bytes 10240 | tf_op jit(solution)/shard_map/all_gather | solution.py:16
  280.7 1.3 select_reduce_fusion
  282.3 1.8 all-gather.20
  284.1 1.8 all-gather.19
  (95 shorter events, 15.7 us)
Async XLA Ops:
  7.2 1.4 copy-start
  7.2 157.0 %all-gather.33.cloned.1.call-start = ((), (), s32[]{:S(2)}) async-start(), calls=%async_computation | async-start | bytes 10485760 | tf_op jit(solution)/shard_map/all_gather | solution.py:90
  8.6 1.0 copy-start.1
  279.7 2.3 copy-start.2
Sparse Core Ops, SparseCore 0:
  11.8 152.3 all-gather.32
